TPU v7x, 32 devices: a whole 2x2x4 slice. The times are simulated.
32 devices in a mesh: dp: 4 (over z), row: 4 (over x, core), col: 2 (over y).
Axes of the slice: x: 2, y: 2, z: 4, core: 2. Of those that a mesh axis runs over, the one named last changes fastest.
Arguments:
- hidden: float32 [4096, 1024], P(('dp', 'row')), may hold values from -6 to 6
- cotangent: float32 [4096, 1024], P(('dp', 'row'), 'col'), may hold values from -6 to 6
- norm_gain: float32 [1024], replicated, may hold values from 0.5 to 1.5
- weight_z: bfloat16 [1024, 2048], P('col', 'row'), may hold values from -0.1875 to 0.1875
- weight_x: bfloat16 [1024, 2048], P('col', 'row'), may hold values from -0.1875 to 0.1875
- weight_dt: bfloat16 [1024, 32], P('col', 'row'), may hold values from -0.1875 to 0.1875
- weight_bc: bfloat16 [1024, 256], P('col'), may hold values from -0.1875 to 0.1875
- conv_weight: float32 [4, 2048], P(None, ('row', 'col')), may hold values from -3 to 3
- conv_bias: float32 [2048], P(('row', 'col')), may hold values from -3 to 3
- bc_conv_weight: float32 [4, 256], replicated, may hold values from -3 to 3
- bc_conv_bias: float32 [256], replicated, may hold values from -3 to 3
- dt_bias: float32 [32], P(('row', 'col')), may hold values from -5 to -1
- decay_log: float32 [32], P(('row', 'col')), may hold values from 0 to 2.77
- skip_gain: float32 [32], P(('row', 'col')), may hold values from 0.5 to 1.5
- gate_gain: float32 [2048], P(('row', 'col')), may hold values from 0.25 to 1.75
- out_weight: bfloat16 [2048, 1024], P('row', 'col'), may hold values from -0.125 to 0.125
Outputs:
- output: float32 [4096, 1024], P(('dp', 'row'), 'col')
- grad_hidden: float32 [4096, 1024], P(('dp', 'row'), 'col')
- grad_norm_gain: float32 [1024], P('col')
- grad_weight_z: float32 [1024, 2048], P('col', 'row')
- grad_weight_x: float32 [1024, 2048], P('col', 'row')
- grad_weight_dt: float32 [1024, 32], P('col', 'row')
- grad_weight_bc: float32 [1024, 256], P('col')
- grad_conv_weight: float32 [4, 2048], P(None, ('row', 'col'))
- grad_conv_bias: float32 [2048], P(('row', 'col'))
- grad_bc_conv_weight: float32 [4, 256], replicated
- grad_bc_conv_bias: float32 [256], replicated
- grad_dt_bias: float32 [32], P(('row', 'col'))
- grad_decay_log: float32 [32], P(('row', 'col'))
- grad_skip_gain: float32 [32], P(('row', 'col'))
- grad_gate_gain: float32 [2048], P(('row', 'col'))
- grad_out_weight: float32 [2048, 1024], P('row', 'col')
All inputs are finite; a program needn't handle non-finite values.
Results may differ from a plain program's by a relative error of at most 0.012.
Values may be sent and summed in bfloat16 or wider, within the bound.
A program may use at most 128 MiB of HBM per device.

v0:
```python
import jax
import jax.numpy as jnp
from jax import lax
from jax.sharding import PartitionSpec as P

BLOCK = 256
SEQ_LEN = 1024
INNER = 2048
EPSILON = 1e-05
PRECISE = lax.Precision.HIGHEST


def causal_conv(values, kernel, offset_bias):
    kernel_width = kernel.shape[0]
    length = values.shape[0]
    padded = jnp.pad(values, ((kernel_width - 1, 0), (0, 0)))
    summed = jnp.broadcast_to(offset_bias[None, :], values.shape)
    for offset in range(kernel_width):
        summed = summed + kernel[offset][None, :] * padded[offset : offset + length]
    return summed


def block_scan(inputs, step_sizes, rates, b_values, c_values):
    length, head_count, head_width = inputs.shape
    block_count = length // BLOCK
    state_width = b_values.shape[1]
    blocks = inputs.reshape(block_count, BLOCK, head_count, head_width)
    block_steps = step_sizes.reshape(block_count, BLOCK, head_count)
    log_decay = jnp.cumsum(block_steps * rates[None, None, :], axis=1)
    b_blocks = b_values.reshape(block_count, BLOCK, state_width)
    c_blocks = c_values.reshape(block_count, BLOCK, state_width)
    scores = jnp.einsum("cln,csn->cls", c_blocks, b_blocks, precision=PRECISE)
    causal = jnp.arange(BLOCK)[:, None] >= jnp.arange(BLOCK)[None, :]
    log_gap = log_decay[:, :, None, :] - log_decay[:, None, :, :]
    decays = jnp.exp(jnp.where(causal[None, :, :, None], log_gap, -1e30))
    mixing = scores[:, :, :, None] * decays * block_steps[:, None, :, :]
    inside = jnp.einsum("clsh,cshp->clhp", mixing, blocks, precision=PRECISE)
    tail_decay = jnp.exp(log_decay[:, -1:, :] - log_decay) * block_steps
    states = jnp.einsum("csn,csh,cshp->chpn", b_blocks, tail_decay, blocks, precision=PRECISE)
    carried = jnp.exp(log_decay[:, -1, :])

    def advance(running, pair_item):
        new_state, factor = pair_item
        return (running * factor[:, None, None] + new_state, running)

    initial = jnp.zeros((head_count, head_width, state_width), jnp.float32)
    _, entering = lax.scan(advance, initial, (states, carried))
    outside = jnp.einsum(
        "cln,chpn,clh->clhp", c_blocks, entering, jnp.exp(log_decay), precision=PRECISE
    )
    return (inside + outside).reshape(length, head_count, head_width)


def sequence_mixer(
    z_raw,
    x_raw,
    step_raw,
    bc_raw,
    conv_weight,
    conv_bias,
    bc_conv_weight,
    bc_conv_bias,
    dt_bias,
    decay_log,
    skip_gain,
):
    x_conv = jax.nn.silu(causal_conv(x_raw, conv_weight, conv_bias))
    bc_conv = jax.nn.silu(causal_conv(bc_raw, bc_conv_weight, bc_conv_bias))
    state_width = bc_conv.shape[1] // 2
    head_count = step_raw.shape[1]
    length = x_conv.shape[0]
    heads_in = x_conv.reshape(length, head_count, -1)
    step_size = jax.nn.softplus(step_raw + dt_bias[None, :])
    rates = -jnp.exp(decay_log)
    mixed = block_scan(
        heads_in, step_size, rates, bc_conv[:, :state_width], bc_conv[:, state_width:]
    )
    mixed = mixed + skip_gain[None, :, None] * heads_in
    return mixed.reshape(length, -1) * jax.nn.silu(z_raw)


def group_mixer(
    z_raw,
    x_raw,
    step_raw,
    bc_raw,
    conv_weight,
    conv_bias,
    bc_conv_weight,
    bc_conv_bias,
    dt_bias,
    decay_log,
    skip_gain,
):
    total_rows = z_raw.shape[0]
    seq_count = total_rows // SEQ_LEN

    def split_seqs(matrix):
        return matrix.reshape(seq_count, SEQ_LEN, matrix.shape[1])

    mapped = jax.vmap(
        sequence_mixer, in_axes=(0, 0, 0, 0, None, None, None, None, None, None, None)
    )
    result = mapped(
        split_seqs(z_raw),
        split_seqs(x_raw),
        split_seqs(step_raw),
        split_seqs(bc_raw),
        conv_weight,
        conv_bias,
        bc_conv_weight,
        bc_conv_bias,
        dt_bias,
        decay_log,
        skip_gain,
    )
    return result.reshape(total_rows, -1)


def body(
    hidden,
    cotangent,
    norm_gain,
    weight_z,
    weight_x,
    weight_dt,
    weight_bc,
    conv_weight,
    conv_bias,
    bc_conv_weight,
    bc_conv_bias,
    dt_bias,
    decay_log,
    skip_gain,
    gate_gain,
    out_weight,
):
    row_count = lax.axis_size("row")
    col_count = lax.axis_size("col")
    row_index = lax.axis_index("row")
    col_index = lax.axis_index("col")
    model_width = hidden.shape[1]
    col_width = weight_z.shape[0]
    chan_width = weight_z.shape[1] // col_count
    head_width = weight_dt.shape[1] // col_count
    bc_width = weight_bc.shape[1]
    slot_width = 2 * chan_width + head_width
    inv_rms = lax.rsqrt(jnp.mean(hidden * hidden, axis=1, keepdims=True) + EPSILON)
    normed = hidden * inv_rms
    normed_col = lax.dynamic_slice_in_dim(normed, col_index * col_width, col_width, 1)
    scaled = (normed * norm_gain[None, :]).astype(jnp.bfloat16)
    scaled_col = lax.dynamic_slice_in_dim(scaled, col_index * col_width, col_width, 1)
    gathered_rows = lax.all_gather(scaled_col, "row", axis=0, tiled=True)
    group_rows = gathered_rows.shape[0]
    head_blocks = jnp.concatenate(
        [
            weight_z.reshape(col_width, col_count, chan_width),
            weight_x.reshape(col_width, col_count, chan_width),
            weight_dt.reshape(col_width, col_count, head_width),
        ],
        axis=2,
    ).reshape(col_width, col_count * slot_width)
    with_shared = jnp.concatenate(
        [
            head_blocks.reshape(col_width, col_count, slot_width),
            jnp.broadcast_to(weight_bc[:, None, :], (col_width, col_count, bc_width)),
        ],
        axis=2,
    ).reshape(col_width, col_count * (slot_width + bc_width))
    partial_proj = jnp.dot(gathered_rows, with_shared, preferred_element_type=jnp.float32).reshape(
        group_rows, col_count, slot_width + bc_width
    )
    projected = lax.psum_scatter(partial_proj, "col", scatter_dimension=1, tiled=True).reshape(
        group_rows, slot_width + bc_width
    )
    z_raw = projected[:, :chan_width]
    x_raw = projected[:, chan_width : 2 * chan_width]
    step_raw = projected[:, 2 * chan_width : slot_width]
    bc_raw = projected[:, slot_width:]
    gated, pullback = jax.vjp(
        group_mixer,
        z_raw,
        x_raw,
        step_raw,
        bc_raw,
        conv_weight,
        conv_bias,
        bc_conv_weight,
        bc_conv_bias,
        dt_bias,
        decay_log,
        skip_gain,
    )
    square_total = lax.psum(jnp.sum(gated * gated, axis=1), ("row", "col"))
    inv_gate = lax.rsqrt(square_total[:, None] / INNER + EPSILON)
    gate_hat = gated * inv_gate
    gate_out = (gate_hat * gate_gain[None, :]).astype(jnp.bfloat16)
    gate_rows = lax.all_gather(gate_out, "col", axis=1, tiled=True)
    piece = gate_rows
    branch_out = lax.psum_scatter(
        jnp.dot(piece, out_weight, preferred_element_type=jnp.float32),
        "row",
        scatter_dimension=0,
        tiled=True,
    )
    hidden_col = lax.dynamic_slice_in_dim(hidden, col_index * col_width, col_width, 1)
    output = hidden_col + branch_out
    cot_half = cotangent.astype(jnp.bfloat16)
    cot_rows = lax.all_gather(cot_half, "row", axis=0, tiled=True)
    grad_out_weight = lax.dot_general(
        gate_rows, cot_rows, (((0,), (0,)), ((), ())), preferred_element_type=jnp.float32
    )
    chan_part = lax.dot_general(
        cot_rows, out_weight, (((1,), (1,)), ((), ())), preferred_element_type=jnp.float32
    )
    grad_gate_out = lax.psum_scatter(chan_part, "col", scatter_dimension=1, tiled=True)
    grad_gate_gain = jnp.sum(grad_gate_out * gate_hat, axis=0)
    grad_hat = grad_gate_out * gate_gain[None, :]
    gate_dot = lax.psum(jnp.sum(grad_hat * gate_hat, axis=1), ("row", "col"))
    grad_gated = inv_gate * (grad_hat - gate_hat * (gate_dot[:, None] / INNER))
    (
        grad_z,
        grad_x,
        grad_step,
        grad_bc,
        grad_conv_weight,
        grad_conv_bias,
        grad_bc_conv_weight,
        grad_bc_conv_bias,
        grad_dt_bias,
        grad_decay_log,
        grad_skip_gain,
    ) = pullback(grad_gated)
    bc_total = lax.psum(grad_bc, "col")
    grad_slot = jnp.concatenate([grad_z, grad_x, grad_step], axis=1).astype(jnp.bfloat16)
    grad_cols = lax.all_gather(grad_slot, "col", axis=1, tiled=True)
    bc_wide = weight_bc.astype(jnp.float32)
    piece = grad_cols
    heads_term = lax.dot_general(
        piece, head_blocks, (((1,), (1,)), ((), ())), preferred_element_type=jnp.float32
    )
    grad_scaled = lax.psum_scatter(
        heads_term + jnp.dot(bc_total, bc_wide.T, precision=PRECISE),
        "row",
        scatter_dimension=0,
        tiled=True,
    )
    head_grads = lax.dot_general(
        gathered_rows, grad_cols, (((0,), (0,)), ((), ())), preferred_element_type=jnp.float32
    ).reshape(col_width, col_count, slot_width)
    grad_weight_z = head_grads[:, :, :chan_width].reshape(col_width, col_count * chan_width)
    grad_weight_x = head_grads[:, :, chan_width : 2 * chan_width].reshape(
        col_width, col_count * chan_width
    )
    grad_weight_dt = head_grads[:, :, 2 * chan_width :].reshape(col_width, col_count * head_width)
    bc_part = jnp.dot(gathered_rows.astype(jnp.float32).T, bc_total, precision=PRECISE)
    gain_col = lax.dynamic_slice_in_dim(norm_gain, col_index * col_width, col_width, 0)
    gain_part = jnp.sum(grad_scaled * normed_col, axis=0)
    grad_in = grad_scaled * gain_col[None, :]
    input_dot = jnp.sum(grad_in * normed_col, axis=1)
    row_hot = (jnp.arange(row_count) == row_index).astype(jnp.float32)
    col_hot = (jnp.arange(col_count) == col_index).astype(jnp.float32)
    dot_slots, gain_slots, bc_slots, bc_weight_sum, bc_bias_sum = lax.psum(
        (
            row_hot[:, None] * input_dot[None, :],
            col_hot[:, None] * gain_part[None, :],
            col_hot[:, None, None] * bc_part[None, :, :],
            grad_bc_conv_weight,
            grad_bc_conv_bias,
        ),
        ("row", "col"),
    )
    input_total = lax.dynamic_index_in_dim(dot_slots, row_index, 0, keepdims=False)
    gain_mine = lax.dynamic_index_in_dim(gain_slots, col_index, 0, keepdims=False)
    bc_mine = lax.dynamic_index_in_dim(bc_slots, col_index, 0, keepdims=False)
    grad_hidden = cotangent + inv_rms * (
        grad_in - normed_col * (input_total[:, None] / model_width)
    )
    summed = lax.psum(
        (
            gain_mine,
            grad_weight_z,
            grad_weight_x,
            grad_weight_dt,
            bc_mine,
            grad_conv_weight,
            grad_conv_bias,
            bc_weight_sum,
            bc_bias_sum,
            grad_dt_bias,
            grad_decay_log,
            grad_skip_gain,
            grad_gate_gain,
            grad_out_weight,
        ),
        "dp",
    )
    return (
        output,
        grad_hidden,
        summed[0],
        summed[1],
        summed[2],
        summed[3],
        summed[4],
        summed[5],
        summed[6],
        summed[7],
        summed[8],
        summed[9],
        summed[10],
        summed[11],
        summed[12],
        summed[13],
    )


def solution(mesh):
    in_specs = (
        P(("dp", "row"), None),
        P(("dp", "row"), "col"),
        P(),
        P("col", "row"),
        P("col", "row"),
        P("col", "row"),
        P("col", None),
        P(None, ("row", "col")),
        P(("row", "col")),
        P(),
        P(),
        P(("row", "col")),
        P(("row", "col")),
        P(("row", "col")),
        P(("row", "col")),
        P("row", "col"),
    )
    out_specs = (
        P(("dp", "row"), "col"),
        P(("dp", "row"), "col"),
        P("col"),
        P("col", "row"),
        P("col", "row"),
        P("col", "row"),
        P("col", None),
        P(None, ("row", "col")),
        P(("row", "col")),
        P(),
        P(),
        P(("row", "col")),
        P(("row", "col")),
        P(("row", "col")),
        P(("row", "col")),
        P("row", "col"),
    )
    return jax.shard_map(body, mesh=mesh, in_specs=in_specs, out_specs=out_specs, check_vma=False)
```

profile of v0, /device:TPU:0, one launch (start us, length us, event | category | flops | bytes accessed | tf_op | source)
XLA Modules:
  0.0 656.2 jit_solution(7282166113597032252)
XLA Ops:
  19.4 11.9 %all-gather.6.cloned.1.call-done = bf16[1024,512]{1,0:T(8,128)(2,1)} async-done(((bf16[256,512]{1,0:T(8,128)(2,1)}), bf16[1024,512]{1,0:T(8,128)(2,1)}) %all-gather.6.cloned.1.call-update) | async-done | bytes 1048592 | tf_op jit(solution)/shard_map/all_gather | solution.py:153
  31.2 5.8 fusion.42
  38.6 11.5 %all-gather.10.cloned.1.call-done = bf16[1024,512]{1,0:T(8,128)(2,1)} async-done(((bf16[256,512]{1,0:T(8,128)(2,1)}), bf16[1024,512]{1,0:T(8,128)(2,1)}) %all-gather.10.cloned.1.call-update) | async-done | bytes 1048592 | tf_op jit(solution)/shard_map/all_gather | solution.py:209
  50.1 3.3 fusion.97
  53.5 76.8 %reduce-scatter.5.cloned.1.call-done = f32[1024,1,772]{0,2,1:T(8,128)} async-done(((f32[1024,2,772]{0,2,1:T(8,128)}), f32[1024,1,772]{0,2,1:T(8,128)}) %reduce-scatter.5.cloned.1.call-update) | async-done | bytes 3162128 | tf_op jit(solution)/shard_map/reduce_scatter | solution.py:173
  131.3 4.8 reduce-window.14
  137.3 2.4 slice_bitcast_fusion.1
  140.8 3.5 fusion.46
  146.1 2.5 fusion.92
  150.8 2.2 copy.254
  153.1 2.1 reshape.668
  157.2 2.1 copy.255
  159.3 3.1 fusion.95
  164.4 11.6 %while.34 = (s32[]{:T(128)}, f32[1,4,64,128]{3,2,1,0:T(8,128)S(1)}, f32[4,1,4,64,128]{4,3,2,1,0:T(8,128)S(1)}, f32[4,1,4,1,1]{2,4,3,1,0:T(1,128)}, f32[4,1,4]{2,...) while((s32[]{:T(128)}, f32[1,4,64,128]{3,2,1,0:T(8,128)S(1)}, ...), condition=%wide.region_5.6_spmd.clone, body=%wide.region_4.5_spmd.clone.sunk | while | flops 131075 | bytes 656552 | solution.py:47
  178.0 6.5 fusion.23
  188.3 12.0 %psum.154 = f32[1024]{0:T(1024)S(1)} all-reduce(f32[1024]{0:T(1024)S(1)} %get-tuple-element.382), channel_id=1, replica_groups=mesh['dp'=4,'row'=4,'col'=2] {'row','col'}, use_global_device_ids=true, to_apply=%region_7.8 | all-reduce | flops 1024 | bytes 8192 | tf_op jit(solution)/shard_map/psum | solution.py:194
  202.5 14.0 %psum.155 = f32[1024]{0:T(1024)S(1)} all-reduce(f32[1024]{0:T(1024)S(1)} %get-tuple-element.312), channel_id=1, replica_groups=mesh['dp'=4,'row'=4,'col'=2] {'row','col'}, use_global_device_ids=true, to_apply=%region_11.12 | all-reduce | flops 1024 | bytes 8192 | tf_op jit(solution)/shard_map/psum | solution.py:219
  216.5 3.2 fusion.35
  225.0 2.7 convolution_bitcast_fusion.4
  230.6 11.7 %while.35 = (s32[]{:T(128)}, f32[1,4,64,128]{3,2,1,0:T(8,128)S(1)}, f32[4,1,4,64,128]{4,3,2,1,0:T(8,128)}, f32[4,1,4]{2,1,0:T(1,128)}, f32[4,1,4,64,128]{4,3,2,1...) while((s32[]{:T(128)}, f32[1,4,64,128]{3,2,1,0:T(8,128)S(1)}, ...), condition=%wide.region_14.15_spmd.clone, body=%wide.region_12.14_spmd.clone.sunk | while | flops 196608 | bytes 787172 | solution.py:47
  242.3 2.3 convolution_bitcast_fusion
  245.5 4.7 fusion.22
  250.2 6.7 %fusion.7 = (f32[4,256,4]{1,2,0:T(4,128)S(1)}, f32[4,256,4]{1,2,0:T(4,128)S(1)}, f32[4,256,4]{1,2,0:T(4,128)S(1)}, f32[4,256,256]{2,1,0:T(8,128)S(1)}) fusion(f32[4,256,4]{1,2,0:T(4,128)S(1)} %bitcast.366, f32[4,256,4]{1,2,0:T(4,128)S(1)} %copy-done.46, f32[4,256,256]{2,1,0:T(8,128)S(1)} %copy-done.35, pred[256,256]{1,0:T(8,128)(4,1)S(1)} %copy-done.45, ...), kind=kOutput, calls=%fused_computation.22 | convolution fusion | flops 818663424 | bytes 4341760 | tf_op jit(solution)/shard_map/transpose(jvp(vmap(clsh,cshp->clhp)))/dot_general | solution.py:37
  262.8 2.6 fusion.25
  265.5 2.1 copy.235
  268.1 3.2 multiply_reduce_fusion.7
  271.4 2.6 broadcast_multiply_fusion.1
  277.2 20.1 %reduce-window.16 = f32[1,4,4,2,128]{4,3,2,1,0:T(2,128)S(1)} reduce-window(f32[1,4,4,2,128]{4,3,2,1,0:T(2,128)S(1)} %reshape.690, f32[]{:T(128)} %constant.120.clone.1), window={size=1x1x1x1x128 pad=0_0x0_0x0_0x0_0x0_127}, to_apply=%region_19.20 | reduce-window | flops 520192 | bytes 32772 | tf_op jit(solution)/shard_map/reduce-window.2
  297.5 3.5 fusion.28
  301.4 3.3 fusion.55
  307.1 9.0 %all-reduce.29.cloned.1.call-done = f32[1024,256]{0,1:T(8,128)} async-done(((f32[1024,256]{0,1:T(8,128)}), f32[1024,256]{0,1:T(8,128)}) %all-reduce.29.cloned.1.call-update) | async-done | bytes 1048592 | tf_op jit(solution)/shard_map/psum | solution.py:234
  316.1 2.5 fusion.100
  319.8 19.6 %all-gather.8.cloned.1.call-done = bf16[1024,512]{0,1:T(8,128)(2,1)} async-done(((bf16[1024,256]{0,1:T(8,128)(2,1)}), bf16[1024,512]{0,1:T(8,128)(2,1)}) %all-gather.8.cloned.1.call-update) | async-done | bytes 1048592 | tf_op jit(solution)/shard_map/all_gather | solution.py:198
  339.4 3.3 fusion.96
  344.3 30.2 %all-gather.12.cloned.1.call-done = bf16[2,516,1024]{2,1,0:T(8,128)(2,1)} async-done(((bf16[1,516,1024]{2,1,0:T(8,128)(2,1)}), bf16[2,516,1024]{2,1,0:T(8,128)(2,1)}) %all-gather.12.cloned.1.call-update) | async-done | bytes 2113552 | tf_op jit(solution)/shard_map/all_gather | solution.py:236
  374.4 3.4 reshape.705
  377.8 3.2 fusion.98
  381.1 3.3 convolution_add_fusion
  384.4 3.0 fusion.101
  387.4 47.5 %all-reduce.31.cloned.1.call-done = f32[2,512,256]{2,1,0:T(8,128)} async-done(((f32[2,512,256]{2,1,0:T(8,128)}), f32[2,512,256]{2,1,0:T(8,128)}) %all-reduce.31.cloned.1.call-update) | async-done | bytes 1048592 | tf_op jit(solution)/shard_map/psum | solution.py:263
  436.8 4.2 fusion.99
  441.0 3.5 reshape.700
  450.6 17.2 %reduce-scatter.7.cloned.1.call-done = f32[256,512]{1,0:T(8,128)} async-done(((f32[1024,512]{1,0:T(8,128)}), f32[256,512]{1,0:T(8,128)}) %reduce-scatter.7.cloned.1.call-update) | async-done | bytes 524304 | tf_op jit(solution)/shard_map/reduce_scatter | solution.py:200
  469.8 31.7 %reduce-scatter.11.cloned.1.call-done = f32[256,512]{1,0:T(8,128)} async-done(((f32[1024,512]{1,0:T(8,128)}), f32[256,512]{1,0:T(8,128)}) %reduce-scatter.11.cloned.1.call-update) | async-done | bytes 524304 | tf_op jit(solution)/shard_map/reduce_scatter | solution.py:242
  502.8 24.5 %all-reduce.22 = (f32[4,256]{1,0:T(4,128)S(1)}, f32[2,512]{1,0:T(2,128)S(1)}, f32[4,256]{1,0:T(4,128)S(1)}, f32[256]{0:T(256)S(1)}) all-reduce(f32[4,256]{1,0:T(4,128)S(1)} %broadcast_multiply_fusion.11, f32[2,512]{1,0:T(2,128)S(1)} %broadcast_multiply_fusion.10, ...), channel_id=1, replica_groups=mesh['dp'=4,'row'=4,'col'=2] {'row','col'}, use_global_device_ids=true, to_apply=%region_25.26 | all-reduce | flops 3328 | bytes 26624 | tf_op jit(solution)/shard_map/psum | solution.py:263
  527.4 21.7 %all-reduce.23 = (f32[512]{0:T(512)}, f32[512,8]{0,1:T(8,128)}, f32[4,256]{1,0:T(4,128)}, f32[256]{0:T(256)}, f32[4,256]{1,0:T(4,128)}, /*index=5*/f32[256]{0:T(...) all-reduce(f32[512]{0:T(512)S(1)} %bitcast.389, ...), channel_id=1, replica_groups=mesh['dp'=4,'row'=4,'col'=2] {'dp'}, use_global_device_ids=true, to_apply=%region_28.29 | all-reduce | flops 7436 | bytes 59488 | tf_op jit(solution)/shard_map/psum | solution.py:279
  551.1 93.3 %all-reduce.33.cloned.1.call-done = (f32[512,512]{1,0:T(8,128)}, f32[512,512]{1,0:T(8,128)}, f32[512,256]{1,0:T(8,128)}, f32[512,512]{1,0:T(8,128)}) async-done(((f32[512,512]{1,0:T(8,128)}, f32[512,512]{1,0:T(8,128)}, f32[512,256]{1,0:T(8,128)}, f32[512,512]{1,0:T(8,128)}), (f32[512,512]{1,0:T(8,128)}, f32[512,512]{1,0:T(8,128)}, f32[512,256]{1,0:T(8,128)}, ...) | async-done | bytes 3670032 | tf_op jit(solution)/shard_map/psum | solution.py:279
  644.4 2.4 copy.363
  (327 shorter events, 95.6 us)
Async XLA Ops:
  7.2 42.9 %copy-start = (bf16[512,512]{1,0:T(8,128)(2,1)S(1)}, bf16[512,512]{1,0:T(8,128)(2,1)}, u32[]{:S(2)}) copy-start(bf16[512,512]{1,0:T(8,128)(2,1)} %param.35) | copy-start | bytes 1572868
  7.2 4.5 copy-start.27
  7.2 24.0 %all-gather.6.cloned.1.call-start = ((), (), s32[]{:S(2)}) async-start(), calls=%async_computation.4 | async-start | bytes 1310720 | tf_op jit(solution)/shard_map/all_gather | solution.py:153
  10.8 4.0 copy-start.14
  11.7 38.4 %all-gather.10.cloned.1.call-start = ((), (), s32[]{:S(2)}) async-start(), calls=%async_computation.8 | async-start | bytes 1310720 | tf_op jit(solution)/shard_map/all_gather | solution.py:209
  12.5 117.8 %reduce-scatter.5.cloned.1.call-start = ((), (), s32[]{:S(2)}) async-start(), calls=%async_computation.5 | async-start | bytes 9535488 | tf_op jit(solution)/shard_map/reduce_scatter | solution.py:173
  37.1 163.3 %reduce-scatter.9.cloned.1.call-start = ((), (), s32[]{:S(2)}) async-start(), calls=%async_computation.9 | async-start | bytes 3145728 | tf_op jit(solution)/shard_map/reduce_scatter | solution.py:216
  38.5 139.6 %copy-start.44 = (pred[256,256]{1,0:T(8,128)(4,1)}, pred[256,256]{1,0:T(8,128)(4,1)S(1)}, u32[]{:S(2)}) copy-start(pred[256,256]{1,0:T(8,128)(4,1)S(1)} %iota_compare_fusion) | copy-start | bytes 196612
  38.5 92.7 %copy-start.75 = (f32[4]{0:T(128)}, f32[4]{0:T(128)S(1)}, u32[]{:S(2)}) copy-start(f32[4]{0:T(128)S(1)} %exponential_negate_fusion) | copy-start | bytes 52
  38.5 102.2 %copy-start.52 = (f32[1,256]{1,0:T(1,128)}, f32[1,256]{1,0:T(1,128)S(1)}, u32[]{:S(2)}) copy-start(f32[1,256]{1,0:T(1,128)S(1)} %get-tuple-element.412) | copy-start | bytes 3076
  38.5 102.2 %copy-start.54 = (f32[1,256]{1,0:T(1,128)}, f32[1,256]{1,0:T(1,128)S(1)}, u32[]{:S(2)}) copy-start(f32[1,256]{1,0:T(1,128)S(1)} %get-tuple-element.413) | copy-start | bytes 3076
  38.6 102.2 %copy-start.56 = (f32[1,256]{1,0:T(1,128)}, f32[1,256]{1,0:T(1,128)S(1)}, u32[]{:S(2)}) copy-start(f32[1,256]{1,0:T(1,128)S(1)} %get-tuple-element.414) | copy-start | bytes 3076
  38.6 102.2 %copy-start.58 = (f32[1,256]{1,0:T(1,128)}, f32[1,256]{1,0:T(1,128)S(1)}, u32[]{:S(2)}) copy-start(f32[1,256]{1,0:T(1,128)S(1)} %get-tuple-element.415) | copy-start | bytes 3076
  38.6 102.2 %copy-start.60 = (f32[1,256]{1,0:T(1,128)}, f32[1,256]{1,0:T(1,128)S(1)}, u32[]{:S(2)}) copy-start(f32[1,256]{1,0:T(1,128)S(1)} %get-tuple-element.416) | copy-start | bytes 3076
  38.6 102.2 %copy-start.62 = (f32[1,256]{1,0:T(1,128)}, f32[1,256]{1,0:T(1,128)S(1)}, u32[]{:S(2)}) copy-start(f32[1,256]{1,0:T(1,128)S(1)} %get-tuple-element.417) | copy-start | bytes 3076
  38.6 102.2 %copy-start.64 = (f32[1,256]{1,0:T(1,128)}, f32[1,256]{1,0:T(1,128)S(1)}, u32[]{:S(2)}) copy-start(f32[1,256]{1,0:T(1,128)S(1)} %get-tuple-element.418) | copy-start | bytes 3076
  38.6 102.2 %copy-start.66 = (f32[1,256]{1,0:T(1,128)}, f32[1,256]{1,0:T(1,128)S(1)}, u32[]{:S(2)}) copy-start(f32[1,256]{1,0:T(1,128)S(1)} %get-tuple-element.419) | copy-start | bytes 3076
  38.6 91.7 %copy-start.73 = (f32[4]{0:T(128)S(1)}, f32[4]{0:T(128)}, u32[]{:S(2)}) copy-start(f32[4]{0:T(128)} %param.31) | copy-start | bytes 52
  53.4 262.7 %all-reduce.29.cloned.1.call-start = ((), (), s32[]{:S(2)}) async-start(), calls=%async_computation.10 | async-start | bytes 2097152 | tf_op jit(solution)/shard_map/psum | solution.py:234
  139.7 4.7 copy-start.9
  139.7 4.7 copy-start.11
  146.1 32.0 %copy-start.5 = (f32[4,256,4,64]{1,0,3,2:T(4,128)}, f32[4,256,4,64]{1,0,3,2:T(4,128)S(1)}, u32[]{:S(2)}) copy-start(f32[4,256,4,64]{1,0,3,2:T(4,128)S(1)} %reshape.666) | copy-start | bytes 3145732
  150.8 11.5 %copy-start.16 = (f32[4,256,128]{2,1,0:T(8,128)}, f32[4,256,128]{2,1,0:T(8,128)S(1)}, u32[]{:S(2)}) copy-start(f32[4,256,128]{2,1,0:T(8,128)S(1)} %copy.216) | copy-start | bytes 1572868
  178.0 6.5 copy-start.24
  185.4 15.0 %copy-start.48 = (f32[256]{0:T(256)S(1)}, f32[256]{0:T(256)}, u32[]{:S(2)}) copy-start(f32[256]{0:T(256)} %param.34) | copy-start | bytes 3076
  188.3 28.1 %copy-start.3 = (f32[1024,256]{0,1:T(8,128)}, f32[1024,256]{0,1:T(8,128)S(1)}, u32[]{:S(2)}) copy-start(f32[1024,256]{0,1:T(8,128)S(1)} %get-tuple-element.383) | copy-start | bytes 3145732
  250.2 6.8 %copy-start.21 = (f32[4,256,128]{2,1,0:T(8,128)S(1)}, f32[4,256,128]{2,1,0:T(8,128)}, u32[]{:S(2)}) copy-start(f32[4,256,128]{2,1,0:T(8,128)} %copy.215) | copy-start | bytes 1572868
  262.8 5.0 copy-start.12
  262.8 5.0 copy-start.26
  274.0 23.5 %copy-start.4 = (f32[1024,256]{0,1:T(8,128)S(1)}, f32[1024,256]{0,1:T(8,128)}, u32[]{:S(2)}) copy-start(f32[1024,256]{0,1:T(8,128)} %copy-done.3) | copy-start | bytes 3145732
  274.0 23.5 %copy-start.49 = (f32[256]{0:T(256)S(1)}, f32[256]{0:T(256)}, u32[]{:S(2)}) copy-start(f32[256]{0:T(256)} %param.34) | copy-start | bytes 3076
  275.9 63.5 %all-gather.8.cloned.1.call-start = ((), (), s32[]{:S(2)}) async-start(), calls=%async_computation.6 | async-start | bytes 1572864 | tf_op jit(solution)/shard_map/all_gather | solution.py:198
  301.0 73.4 %all-gather.12.cloned.1.call-start = ((), (), s32[]{:S(2)}) async-start(), calls=%async_computation.13 | async-start | bytes 3194880 | tf_op jit(solution)/shard_map/all_gather | solution.py:236
  304.7 11.4 %copy-start.33 = (bf16[1024,512]{1,0:T(8,128)(2,1)S(1)}, bf16[1024,512]{1,0:T(8,128)(2,1)}, u32[]{:S(2)}) copy-start(bf16[1024,512]{1,0:T(8,128)(2,1)} %all-gather.6.cloned.1.call-done) | copy-start | bytes 3145732
  307.1 127.8 %all-reduce.31.cloned.1.call-start = ((), (), s32[]{:S(2)}) async-start(), calls=%async_computation.12 | async-start | bytes 2097152 | tf_op jit(solution)/shard_map/psum | solution.py:263
  319.7 23.2 %copy-start.19 = (bf16[512,512]{0,1:T(8,128)(2,1)S(1)}, bf16[512,512]{0,1:T(8,128)(2,1)}, u32[]{:S(2)}) copy-start(bf16[512,512]{0,1:T(8,128)(2,1)} %copy.282) | copy-start | bytes 1572868
  319.8 23.2 %copy-start.20 = (bf16[512,512]{0,1:T(8,128)(2,1)S(1)}, bf16[512,512]{0,1:T(8,128)(2,1)}, u32[]{:S(2)}) copy-start(bf16[512,512]{0,1:T(8,128)(2,1)} %copy.283) | copy-start | bytes 1572868
  319.8 148.1 %reduce-scatter.7.cloned.1.call-start = ((), (), s32[]{:S(2)}) async-start(), calls=%async_computation.7 | async-start | bytes 2621440 | tf_op jit(solution)/shard_map/reduce_scatter | solution.py:200
  342.7 158.7 %reduce-scatter.11.cloned.1.call-start = ((), (), s32[]{:S(2)}) async-start(), calls=%async_computation.11 | async-start | bytes 2621440 | tf_op jit(solution)/shard_map/reduce_scatter | solution.py:242
  344.3 33.5 %copy-start.31 = (bf16[512,1032]{0,1:T(8,128)(2,1)S(1)}, bf16[512,1032]{0,1:T(8,128)(2,1)}, u32[]{:S(2)}) copy-start(bf16[512,1032]{0,1:T(8,128)(2,1)} %reshape.696) | copy-start | bytes 3170308
  384.4 260.0 %all-reduce.33.cloned.1.call-start = ((), (), s32[]{:S(2)}) async-start(), calls=%async_computation.14 | async-start | bytes 7340032 | tf_op jit(solution)/shard_map/psum | solution.py:279
  384.4 52.4 %copy-start.34 = (bf16[1024,512]{1,0:T(8,128)(2,1)S(1)}, bf16[1024,512]{1,0:T(8,128)(2,1)}, u32[]{:S(2)}) copy-start(bf16[1024,512]{1,0:T(8,128)(2,1)} %all-gather.6.cloned.1.call-done) | copy-start | bytes 3145732
  448.9 18.9 %copy-start.13 = (f32[256,1024]{1,0:T(8,128)S(1)}, f32[256,1024]{1,0:T(8,128)}, u32[]{:S(2)}) copy-start(f32[256,1024]{1,0:T(8,128)} %param.20) | copy-start | bytes 3145732
  448.9 52.5 %copy-start.15 = (f32[256,1024]{1,0:T(8,128)S(1)}, f32[256,1024]{1,0:T(8,128)}, u32[]{:S(2)}) copy-start(f32[256,1024]{1,0:T(8,128)} %copy-done.14) | copy-start | bytes 3145732
  449.0 78.4 %copy-start.69 = (f32[256]{0:T(256)S(1)}, f32[256]{0:T(256)}, u32[]{:S(2)}) copy-start(f32[256]{0:T(256)} %get-tuple-element.311) | copy-start | bytes 3076
  449.0 100.1 %copy-start.28 = (f32[256,512]{1,0:T(8,128)S(1)}, f32[256,512]{1,0:T(8,128)}, u32[]{:S(2)}) copy-start(f32[256,512]{1,0:T(8,128)} %param.21) | copy-start | bytes 1572868
  449.0 100.1 %copy-start.51 = (f32[256]{0:T(256)S(1)}, f32[256]{0:T(256)}, u32[]{:S(2)}) copy-start(f32[256]{0:T(256)} %copy-done.50) | copy-start | bytes 3076
  644.4 4.2 copy-start.36
  (46 other events, 123.8 us)
Sparse Core Ops, SparseCore 0:
  11.8 19.4 all-gather.5
  33.4 16.6 all-gather.9
  52.4 77.8 reduce-scatter.4
  132.4 31.9 reduce-scatter.8
  276.0 40.0 all-reduce.28
  318.1 21.2 all-gather.7
  340.9 33.4 all-gather.11
  378.2 56.6 all-reduce.30
  437.4 30.4 reduce-scatter.6
  470.3 31.1 reduce-scatter.10
  505.2 139.0 all-reduce.32
where the time goes:
time: 666 us; the launch traced here: 656 us
  waiting for transfers between devices  349 us (52%)
  other arithmetic  80.2 us (12%)
  blocking collectives  72.2 us (11%)
  local copies, waits for them, and re-layouts  71.6 us (11%)
  matrix products  67.1 us (10%)
  between operations  15.3 us (2%)
    psum x1, waiting for transfers between devices, body(): lax.psum((gain_mine, grad_weight_z, grad_weight_x, grad_weight_dt, bc_min...  93.3 us
    reduce_scatter x1, waiting for transfers between devices, body(): lax.psum_scatter(partial_proj, 'col', scatter_dimension=1, tiled=True)  76.8 us
    psum x1, waiting for transfers between devices, body(): lax.psum((row_hot[:, None] * input_dot[None, :], col_hot[:, None] * gain_...  47.5 us
    reduce_scatter x1, waiting for transfers between devices, body(): lax.psum_scatter(heads_term + jnp.dot(bc_total, bc_wide.T, precision=PREC...  31.7 us
    all_gather x1, waiting for transfers between devices, body(): grad_cols = lax.all_gather(grad_slot, 'col', axis=1, tiled=True)  30.2 us
    another operation x9, other arithmetic  28.7 us
    psum x1, blocking collectives, body(): lax.psum((row_hot[:, None] * input_dot[None, :], col_hot[:, None] * gain_...  24.5 us
    psum x1, blocking collectives, body(): lax.psum((gain_mine, grad_weight_z, grad_weight_x, grad_weight_dt, bc_min...  21.7 us
  transfers between devices with their start and end apart: 11, of which 10 were waited for; matrix products, arithmetic and copies ran while one was open for 22% of the time, Pallas kernels for 0%

commit v1 on v0

--- a/solution.py
+++ b/solution.py
@@ -261,14 +261,17 @@
     row_hot = (jnp.arange(row_count) == row_index).astype(jnp.float32)
     col_hot = (jnp.arange(col_count) == col_index).astype(jnp.float32)
     dot_slots, gain_slots, bc_slots, bc_weight_sum, bc_bias_sum = lax.psum(
-        (
-            row_hot[:, None] * input_dot[None, :],
-            col_hot[:, None] * gain_part[None, :],
-            col_hot[:, None, None] * bc_part[None, :, :],
-            grad_bc_conv_weight,
-            grad_bc_conv_bias,
+        lax.psum(
+            (
+                row_hot[:, None] * input_dot[None, :],
+                col_hot[:, None] * gain_part[None, :],
+                col_hot[:, None, None] * bc_part[None, :, :],
+                grad_bc_conv_weight,
+                grad_bc_conv_bias,
+            ),
+            "col",
         ),
-        ("row", "col"),
+        "row",
     )
     input_total = lax.dynamic_index_in_dim(dot_slots, row_index, 0, keepdims=False)
     gain_mine = lax.dynamic_index_in_dim(gain_slots, col_index, 0, keepdims=False)

time: 666 us -> 687 us (1.032)
  waiting for transfers between devices: 349 us -> 381 us
    psum x1, waiting for transfers between devices: 47.5 us -> 9.97 us  [body(): lax.psum((row_hot[:, None] * input_dot[None, :], col_hot[:, None] * gain_...]
    psum x1, waiting for transfers between devices: 8.98 us -> 37.3 us  [body(): bc_total = lax.psum(grad_bc, 'col')]
    psum x1, blocking collectives: 24.5 us -> 8.12 us  [body(): lax.psum((row_hot[:, None] * input_dot[None, :], col_hot[:, None] * gain_...]
    psum x0 -> x1, waiting for transfers between devices: none -> 16 us  [body(): lax.psum(lax.psum((row_hot[:, None] * input_dot[None, :], col_hot[:, None...]
    reduce_scatter x1, waiting for transfers between devices: 17.2 us -> 31.5 us  [body(): lax.psum_scatter(jnp.dot(piece, out_weight, preferred_element_type=jnp.fl...]
    psum x0 -> x1, blocking collectives: none -> 10.9 us  [body(): lax.psum(lax.psum((row_hot[:, None] * input_dot[None, :], col_hot[:, None...]
  transfers between devices with their start and end apart: 11 -> 12, of which waited for: 10 -> 11; matrix products, arithmetic and copies ran while one was open for 22% -> 21% of each run, Pallas kernels for 0% -> 0%
where the time goes in v1:
time: 687 us; the launch traced here: 678 us
  waiting for transfers between devices  381 us (55%)
  other arithmetic  79.3 us (12%)
  matrix products  68.8 us (10%)
  blocking collectives  66.3 us (10%)
  local copies, waits for them, and re-layouts  65.5 us (10%)
  between operations  15.8 us (2%)
    psum x1, waiting for transfers between devices, body(): lax.psum((gain_mine, grad_weight_z, grad_weight_x, grad_weight_dt, bc_min...  98.9 us
    reduce_scatter x1, waiting for transfers between devices, body(): lax.psum_scatter(partial_proj, 'col', scatter_dimension=1, tiled=True)  76.9 us
    psum x1, waiting for transfers between devices, body(): bc_total = lax.psum(grad_bc, 'col')  37.3 us
    reduce_scatter x1, waiting for transfers between devices, body(): lax.psum_scatter(heads_term + jnp.dot(bc_total, bc_wide.T, precision=PREC...  31.6 us
    reduce_scatter x1, waiting for transfers between devices, body(): lax.psum_scatter(jnp.dot(piece, out_weight, preferred_element_type=jnp.fl...  31.5 us
    all_gather x1, waiting for transfers between devices, body(): grad_cols = lax.all_gather(grad_slot, 'col', axis=1, tiled=True)  30.2 us
    another operation x9, other arithmetic  28.7 us
    all_gather x1, waiting for transfers between devices, body(): gate_rows = lax.all_gather(gate_out, 'col', axis=1, tiled=True)  23.3 us
  transfers between devices with their start and end apart: 12, of which 11 were waited for; matrix products, arithmetic and copies ran while one was open for 21% of the time, Pallas kernels for 0%

profile of v1, /device:TPU:0, one launch (start us, length us, event | category | flops | bytes accessed | tf_op | source)
XLA Modules:
  0.0 677.8 jit_solution(13827030400854686539)
XLA Ops:
  17.4 13.4 %all-gather.6.cloned.1.call-done = bf16[1024,512]{1,0:T(8,128)(2,1)} async-done(((bf16[256,512]{1,0:T(8,128)(2,1)}), bf16[1024,512]{1,0:T(8,128)(2,1)}) %all-gather.6.cloned.1.call-update) | async-done | bytes 1048592 | tf_op jit(solution)/shard_map/all_gather | solution.py:153
  30.8 5.8 fusion.42
  38.1 11.5 %all-gather.10.cloned.1.call-done = bf16[1024,512]{1,0:T(8,128)(2,1)} async-done(((bf16[256,512]{1,0:T(8,128)(2,1)}), bf16[1024,512]{1,0:T(8,128)(2,1)}) %all-gather.10.cloned.1.call-update) | async-done | bytes 1048592 | tf_op jit(solution)/shard_map/all_gather | solution.py:209
  49.7 3.3 fusion.97
  53.0 76.9 %reduce-scatter.5.cloned.1.call-done = f32[1024,1,772]{0,2,1:T(8,128)} async-done(((f32[1024,2,772]{0,2,1:T(8,128)}), f32[1024,1,772]{0,2,1:T(8,128)}) %reduce-scatter.5.cloned.1.call-update) | async-done | bytes 3162128 | tf_op jit(solution)/shard_map/reduce_scatter | solution.py:173
  130.9 4.8 reduce-window.14
  136.8 2.4 slice_bitcast_fusion.1
  140.4 3.6 fusion.46
  145.7 2.5 fusion.92
  150.4 2.2 copy.254
  158.8 3.1 fusion.95
  163.9 11.6 %while.34 = (s32[]{:T(128)}, f32[1,4,64,128]{3,2,1,0:T(8,128)S(1)}, f32[4,1,4,64,128]{4,3,2,1,0:T(8,128)S(1)}, f32[4,1,4,1,1]{2,4,3,1,0:T(1,128)}, f32[4,1,4]{2,...) while((s32[]{:T(128)}, f32[1,4,64,128]{3,2,1,0:T(8,128)S(1)}, ...), condition=%wide.region_5.6_spmd.clone, body=%wide.region_4.5_spmd.clone.sunk | while | flops 131075 | bytes 656552 | solution.py:47
  177.6 6.5 fusion.23
  187.8 12.1 %psum.189 = f32[1024]{0:T(1024)S(1)} all-reduce(f32[1024]{0:T(1024)S(1)} %get-tuple-element.386), channel_id=1, replica_groups=mesh['dp'=4,'row'=4,'col'=2] {'row','col'}, use_global_device_ids=true, to_apply=%region_7.8 | all-reduce | flops 1024 | bytes 8192 | tf_op jit(solution)/shard_map/psum | solution.py:194
  202.0 14.0 %psum.190 = f32[1024]{0:T(1024)S(1)} all-reduce(f32[1024]{0:T(1024)S(1)} %get-tuple-element.312), channel_id=1, replica_groups=mesh['dp'=4,'row'=4,'col'=2] {'row','col'}, use_global_device_ids=true, to_apply=%region_11.12 | all-reduce | flops 1024 | bytes 8192 | tf_op jit(solution)/shard_map/psum | solution.py:219
  216.0 3.2 fusion.35
  220.6 3.4 convolution_bitcast_fusion.5
  224.0 2.7 convolution_bitcast_fusion.4
  229.0 9.7 %while.35 = (s32[]{:T(128)}, f32[1,4,64,128]{3,2,1,0:T(8,128)S(1)}, f32[4,1,4,64,128]{4,3,2,1,0:T(8,128)}, f32[4,1,4]{2,1,0:T(1,128)S(1)}, f32[4,1,4,64,128]{4,3...) while((s32[]{:T(128)}, f32[1,4,64,128]{3,2,1,0:T(8,128)S(1)}, ...), condition=%wide.region_14.15_spmd.clone, body=%wide.region_12.14_spmd.clone.sunk | while | flops 196608 | bytes 787668 | solution.py:47
  238.7 2.2 convolution_bitcast_fusion
  241.0 8.7 %fusion.7 = (f32[4,256,4]{1,2,0:T(4,128)S(1)}, f32[4,256,4]{1,2,0:T(4,128)S(1)}, f32[4,256,4]{1,2,0:T(4,128)S(1)}, f32[4,256,256]{2,1,0:T(8,128)S(1)}) fusion(f32[4,256,4]{1,2,0:T(4,128)S(1)} %bitcast.365, f32[4,256,4]{1,2,0:T(4,128)S(1)} %copy-done.46, f32[4,256,256]{2,1,0:T(8,128)} %fusion.95, pred[256,256]{1,0:T(8,128)(4,1)S(1)} %iota_compare_fusion, ...), kind=kOutput, calls=%fused_computation.22 | convolution fusion | flops 818663424 | bytes 4341760 | tf_op jit(solution)/shard_map/transpose(jvp(vmap(clsh,cshp->clhp)))/dot_general | solution.py:37
  249.7 4.7 fusion.22
  260.3 2.6 fusion.25
  265.7 3.2 multiply_reduce_fusion.7
  268.9 2.6 broadcast_multiply_fusion.1
  276.3 37.3 %all-reduce.31.cloned.1.call-done = f32[1024,256]{0,1:T(8,128)} async-done(((f32[1024,256]{0,1:T(8,128)}), f32[1024,256]{0,1:T(8,128)}) %all-reduce.31.cloned.1.call-update) | async-done | bytes 1048592 | tf_op jit(solution)/shard_map/psum | solution.py:234
  313.6 2.8 fusion.100
  318.3 20.1 %reduce-window.16 = f32[1,4,4,2,128]{4,3,2,1,0:T(2,128)S(1)} reduce-window(f32[1,4,4,2,128]{4,3,2,1,0:T(2,128)S(1)} %reshape.690, f32[]{:T(128)} %constant.120.clone.1), window={size=1x1x1x1x128 pad=0_0x0_0x0_0x0_0x0_127}, to_apply=%region_19.20 | reduce-window | flops 520192 | bytes 32772 | tf_op jit(solution)/shard_map/reduce-window.2
  338.6 3.5 fusion.28
  342.5 3.2 fusion.55
  348.0 10.0 %all-reduce.33.cloned.1.call-done = f32[2,512,256]{2,1,0:T(8,128)} async-done(((f32[2,512,256]{2,1,0:T(8,128)}), f32[2,512,256]{2,1,0:T(8,128)}) %all-reduce.33.cloned.1.call-update) | async-done | bytes 1048592 | tf_op jit(solution)/shard_map/psum | solution.py:264
  358.0 23.3 %all-gather.8.cloned.1.call-done = bf16[1024,512]{0,1:T(8,128)(2,1)} async-done(((bf16[1024,256]{0,1:T(8,128)(2,1)}), bf16[1024,512]{0,1:T(8,128)(2,1)}) %all-gather.8.cloned.1.call-update) | async-done | bytes 1048592 | tf_op jit(solution)/shard_map/all_gather | solution.py:198
  381.4 3.3 fusion.96
  386.2 30.2 %all-gather.12.cloned.1.call-done = bf16[2,516,1024]{2,1,0:T(8,128)(2,1)} async-done(((bf16[1,516,1024]{2,1,0:T(8,128)(2,1)}), bf16[2,516,1024]{2,1,0:T(8,128)(2,1)}) %all-gather.12.cloned.1.call-update) | async-done | bytes 2113552 | tf_op jit(solution)/shard_map/all_gather | solution.py:236
  418.4 2.9 fusion.98
  421.3 3.2 convolution_add_fusion
  424.6 3.3 fusion.101
  428.0 2.6 fusion.99
  434.0 2.5 copy.252
  436.5 2.5 copy.251
  439.1 16.0 %all-reduce.35.cloned.1.call-done = f32[2,512,256]{2,1,0:T(8,128)} async-done(((f32[2,512,256]{2,1,0:T(8,128)}), f32[2,512,256]{2,1,0:T(8,128)}) %all-reduce.35.cloned.1.call-update) | async-done | bytes 1048592 | tf_op jit(solution)/shard_map/psum | solution.py:263
  457.6 31.5 %reduce-scatter.7.cloned.1.call-done = f32[256,512]{1,0:T(8,128)} async-done(((f32[1024,512]{1,0:T(8,128)}), f32[256,512]{1,0:T(8,128)}) %reduce-scatter.7.cloned.1.call-update) | async-done | bytes 524304 | tf_op jit(solution)/shard_map/reduce_scatter | solution.py:200
  491.2 31.6 %reduce-scatter.11.cloned.1.call-done = f32[256,512]{1,0:T(8,128)} async-done(((f32[1024,512]{1,0:T(8,128)}), f32[256,512]{1,0:T(8,128)}) %reduce-scatter.11.cloned.1.call-update) | async-done | bytes 524304 | tf_op jit(solution)/shard_map/reduce_scatter | solution.py:242
  524.4 8.1 %all-reduce.25 = (f32[4,256]{1,0:T(4,128)S(1)}, f32[2,512]{1,0:T(2,128)S(1)}, f32[4,256]{1,0:T(4,128)S(1)}, f32[256]{0:T(256)S(1)}) all-reduce(f32[4,256]{1,0:T(4,128)S(1)} %broadcast_multiply_fusion.11, f32[2,512]{1,0:T(2,128)S(1)} %broadcast_multiply_fusion.10, ...), channel_id=1, replica_groups=mesh['dp'=4,'row'=4,'col'=2] {'col'}, use_global_device_ids=true, to_apply=%region_25.26 | all-reduce | flops 3328 | bytes 26624 | tf_op jit(solution)/shard_map/psum | solution.py:264
  532.5 10.9 %all-reduce.22 = (f32[4,256]{1,0:T(4,128)S(1)}, f32[2,512]{1,0:T(2,128)S(1)}, f32[4,256]{1,0:T(4,128)S(1)}, f32[256]{0:T(256)S(1)}) all-reduce(f32[4,256]{1,0:T(4,128)S(1)} %get-tuple-element.376, f32[2,512]{1,0:T(2,128)S(1)} %get-tuple-element.377, ...), channel_id=1, replica_groups=mesh['dp'=4,'row'=4,'col'=2] {'row'}, use_global_device_ids=true, to_apply=%region_26.27 | all-reduce | flops 3328 | bytes 26624 | tf_op jit(solution)/shard_map/psum | solution.py:263
  543.4 21.2 %all-reduce.23 = (f32[512]{0:T(512)}, f32[512,8]{0,1:T(8,128)}, f32[4,256]{1,0:T(4,128)}, f32[256]{0:T(256)}, f32[4,256]{1,0:T(4,128)}, /*index=5*/f32[256]{0:T(...) all-reduce(f32[512]{0:T(512)S(1)} %bitcast.390, ...), channel_id=1, replica_groups=mesh['dp'=4,'row'=4,'col'=2] {'dp'}, use_global_device_ids=true, to_apply=%region_30.31 | all-reduce | flops 7436 | bytes 59488 | tf_op jit(solution)/shard_map/psum | solution.py:282
  566.7 98.9 %all-reduce.37.cloned.1.call-done = (f32[512,512]{1,0:T(8,128)}, f32[512,512]{1,0:T(8,128)}, f32[512,256]{1,0:T(8,128)}, f32[512,512]{1,0:T(8,128)}) async-done(((f32[512,512]{1,0:T(8,128)}, f32[512,512]{1,0:T(8,128)}, f32[512,256]{1,0:T(8,128)}, f32[512,512]{1,0:T(8,128)}), (f32[512,512]{1,0:T(8,128)}, f32[512,512]{1,0:T(8,128)}, f32[512,256]{1,0:T(8,128)}, ...) | async-done | bytes 3670032 | tf_op jit(solution)/shard_map/psum | solution.py:282
  665.6 2.4 copy.364
  (337 shorter events, 94.7 us)
Async XLA Ops:
  7.2 42.5 %copy-start = (bf16[512,512]{1,0:T(8,128)(2,1)S(1)}, bf16[512,512]{1,0:T(8,128)(2,1)}, u32[]{:S(2)}) copy-start(bf16[512,512]{1,0:T(8,128)(2,1)} %param.35) | copy-start | bytes 1572868
  7.2 23.6 %all-gather.6.cloned.1.call-start = ((), (), s32[]{:S(2)}) async-start(), calls=%async_computation.4 | async-start | bytes 1310720 | tf_op jit(solution)/shard_map/all_gather | solution.py:153
  11.2 38.4 %all-gather.10.cloned.1.call-start = ((), (), s32[]{:S(2)}) async-start(), calls=%async_computation.8 | async-start | bytes 1310720 | tf_op jit(solution)/shard_map/all_gather | solution.py:209
  12.1 117.8 %reduce-scatter.5.cloned.1.call-start = ((), (), s32[]{:S(2)}) async-start(), calls=%async_computation.5 | async-start | bytes 9535488 | tf_op jit(solution)/shard_map/reduce_scatter | solution.py:173
  36.6 163.3 %reduce-scatter.9.cloned.1.call-start = ((), (), s32[]{:S(2)}) async-start(), calls=%async_computation.9 | async-start | bytes 3145728 | tf_op jit(solution)/shard_map/reduce_scatter | solution.py:216
  38.0 92.7 %copy-start.78 = (f32[4]{0:T(128)}, f32[4]{0:T(128)S(1)}, u32[]{:S(2)}) copy-start(f32[4]{0:T(128)S(1)} %exponential_negate_fusion) | copy-start | bytes 52
  38.0 102.2 %copy-start.53 = (f32[1,256]{1,0:T(1,128)}, f32[1,256]{1,0:T(1,128)S(1)}, u32[]{:S(2)}) copy-start(f32[1,256]{1,0:T(1,128)S(1)} %get-tuple-element.416) | copy-start | bytes 3076
  38.1 102.2 %copy-start.55 = (f32[1,256]{1,0:T(1,128)}, f32[1,256]{1,0:T(1,128)S(1)}, u32[]{:S(2)}) copy-start(f32[1,256]{1,0:T(1,128)S(1)} %get-tuple-element.417) | copy-start | bytes 3076
  38.1 102.2 %copy-start.57 = (f32[1,256]{1,0:T(1,128)}, f32[1,256]{1,0:T(1,128)S(1)}, u32[]{:S(2)}) copy-start(f32[1,256]{1,0:T(1,128)S(1)} %get-tuple-element.418) | copy-start | bytes 3076
  38.1 102.2 %copy-start.59 = (f32[1,256]{1,0:T(1,128)}, f32[1,256]{1,0:T(1,128)S(1)}, u32[]{:S(2)}) copy-start(f32[1,256]{1,0:T(1,128)S(1)} %get-tuple-element.419) | copy-start | bytes 3076
  38.1 102.2 %copy-start.61 = (f32[1,256]{1,0:T(1,128)}, f32[1,256]{1,0:T(1,128)S(1)}, u32[]{:S(2)}) copy-start(f32[1,256]{1,0:T(1,128)S(1)} %get-tuple-element.420) | copy-start | bytes 3076
  38.1 102.2 %copy-start.63 = (f32[1,256]{1,0:T(1,128)}, f32[1,256]{1,0:T(1,128)S(1)}, u32[]{:S(2)}) copy-start(f32[1,256]{1,0:T(1,128)S(1)} %get-tuple-element.421) | copy-start | bytes 3076
  38.1 102.2 %copy-start.65 = (f32[1,256]{1,0:T(1,128)}, f32[1,256]{1,0:T(1,128)S(1)}, u32[]{:S(2)}) copy-start(f32[1,256]{1,0:T(1,128)S(1)} %get-tuple-element.422) | copy-start | bytes 3076
  38.1 102.2 %copy-start.67 = (f32[1,256]{1,0:T(1,128)}, f32[1,256]{1,0:T(1,128)S(1)}, u32[]{:S(2)}) copy-start(f32[1,256]{1,0:T(1,128)S(1)} %get-tuple-element.423) | copy-start | bytes 3076
  38.1 91.8 %copy-start.76 = (f32[4]{0:T(128)S(1)}, f32[4]{0:T(128)}, u32[]{:S(2)}) copy-start(f32[4]{0:T(128)} %param.31) | copy-start | bytes 52
  53.0 260.6 %all-reduce.31.cloned.1.call-start = ((), (), s32[]{:S(2)}) async-start(), calls=%async_computation.10 | async-start | bytes 2097152 | tf_op jit(solution)/shard_map/psum | solution.py:234
  145.7 31.9 %copy-start.3 = (f32[4,256,4,64]{1,0,3,2:T(4,128)}, f32[4,256,4,64]{1,0,3,2:T(4,128)S(1)}, u32[]{:S(2)}) copy-start(f32[4,256,4,64]{1,0,3,2:T(4,128)S(1)} %reshape.666) | copy-start | bytes 3145732
  150.4 11.5 %copy-start.15 = (f32[4,256,128]{2,1,0:T(8,128)}, f32[4,256,128]{2,1,0:T(8,128)S(1)}, u32[]{:S(2)}) copy-start(f32[4,256,128]{2,1,0:T(8,128)S(1)} %copy.216) | copy-start | bytes 1572868
  177.6 6.5 copy-start.24
  185.0 14.9 %copy-start.49 = (f32[256]{0:T(256)S(1)}, f32[256]{0:T(256)}, u32[]{:S(2)}) copy-start(f32[256]{0:T(256)} %param.34) | copy-start | bytes 3076
  187.8 28.1 %copy-start.5 = (f32[1024,256]{0,1:T(8,128)}, f32[1024,256]{0,1:T(8,128)S(1)}, u32[]{:S(2)}) copy-start(f32[1024,256]{0,1:T(8,128)S(1)} %get-tuple-element.387) | copy-start | bytes 3145732
  229.0 11.9 %copy-start.46 = (f32[4,256,4]{1,2,0:T(4,128)S(1)}, f32[4,256,4]{1,2,0:T(4,128)}, u32[]{:S(2)}) copy-start(f32[4,256,4]{1,2,0:T(4,128)} %add_bitcast_fusion) | copy-start | bytes 49156
  238.7 10.9 %copy-start.69 = (f32[4,1,4]{2,1,0:T(1,128)}, f32[4,1,4]{2,1,0:T(1,128)S(1)}, u32[]{:S(2)}) copy-start(f32[4,1,4]{2,1,0:T(1,128)S(1)} %get-tuple-element.194) | copy-start | bytes 196
  241.0 8.7 %copy-start.25 = (f32[4,256,4,64]{1,3,2,0:T(8,128)}, f32[4,256,4,64]{1,3,2,0:T(8,128)S(1)}, u32[]{:S(2)}) copy-start(f32[4,256,4,64]{1,3,2,0:T(8,128)S(1)} %convolution_bitcast_fusion) | copy-start | bytes 3145732
  241.0 8.7 %copy-start.34 = (f32[4,256,256]{2,1,0:T(8,128)S(1)}, f32[4,256,256]{2,1,0:T(8,128)}, u32[]{:S(2)}) copy-start(f32[4,256,256]{2,1,0:T(8,128)} %fusion.95) | copy-start | bytes 3145732
  241.0 8.7 %copy-start.37 = (f32[1,4,256,4,64]{2,1,4,3,0:T(4,128)S(1)}, f32[1,4,256,4,64]{2,1,4,3,0:T(4,128)}, u32[]{:S(2)}) copy-start(f32[1,4,256,4,64]{2,1,4,3,0:T(4,128)} %reshape.685) | copy-start | bytes 3145732
  249.7 4.7 copy-start.22
  260.3 5.0 copy-start.12
  260.3 5.0 copy-start.28
  273.4 84.5 %all-reduce.33.cloned.1.call-start = ((), (), s32[]{:S(2)}) async-start(), calls=%async_computation.12 | async-start | bytes 2097152 | tf_op jit(solution)/shard_map/psum | solution.py:264
  276.3 41.5 %copy-start.70 = (f32[4,1,4]{2,1,0:T(1,128)S(1)}, f32[4,1,4]{2,1,0:T(1,128)}, u32[]{:S(2)}) copy-start(f32[4,1,4]{2,1,0:T(1,128)} %copy-done.69) | copy-start | bytes 196
  316.5 22.1 %copy-start.6 = (f32[1024,256]{0,1:T(8,128)S(1)}, f32[1024,256]{0,1:T(8,128)}, u32[]{:S(2)}) copy-start(f32[1024,256]{0,1:T(8,128)} %copy-done.5) | copy-start | bytes 3145732
  316.5 22.1 %copy-start.43 = (f32[1024]{0:T(1024)S(1)}, f32[1024]{0:T(1024)}, u32[]{:S(2)}) copy-start(f32[1024]{0:T(1024)} %copy-done.42) | copy-start | bytes 12292
  316.5 22.1 %copy-start.50 = (f32[256]{0:T(256)S(1)}, f32[256]{0:T(256)}, u32[]{:S(2)}) copy-start(f32[256]{0:T(256)} %param.34) | copy-start | bytes 3076
  317.6 63.7 %all-gather.8.cloned.1.call-start = ((), (), s32[]{:S(2)}) async-start(), calls=%async_computation.6 | async-start | bytes 1572864 | tf_op jit(solution)/shard_map/all_gather | solution.py:198
  342.1 74.3 %all-gather.12.cloned.1.call-start = ((), (), s32[]{:S(2)}) async-start(), calls=%async_computation.14 | async-start | bytes 3194880 | tf_op jit(solution)/shard_map/all_gather | solution.py:236
  347.9 107.2 %all-reduce.35.cloned.1.call-start = ((), (), s32[]{:S(2)}) async-start(), calls=%async_computation.13 | async-start | bytes 2097152 | tf_op jit(solution)/shard_map/psum | solution.py:263
  358.0 26.9 %copy-start.19 = (bf16[512,512]{0,1:T(8,128)(2,1)S(1)}, bf16[512,512]{0,1:T(8,128)(2,1)}, u32[]{:S(2)}) copy-start(bf16[512,512]{0,1:T(8,128)(2,1)} %copy-done.18) | copy-start | bytes 1572868
  358.0 26.9 %copy-start.21 = (bf16[512,512]{0,1:T(8,128)(2,1)S(1)}, bf16[512,512]{0,1:T(8,128)(2,1)}, u32[]{:S(2)}) copy-start(bf16[512,512]{0,1:T(8,128)(2,1)} %copy-done.20) | copy-start | bytes 1572868
  358.0 131.1 %reduce-scatter.7.cloned.1.call-start = ((), (), s32[]{:S(2)}) async-start(), calls=%async_computation.7 | async-start | bytes 2621440 | tf_op jit(solution)/shard_map/reduce_scatter | solution.py:200
  384.7 138.2 %reduce-scatter.11.cloned.1.call-start = ((), (), s32[]{:S(2)}) async-start(), calls=%async_computation.11 | async-start | bytes 2621440 | tf_op jit(solution)/shard_map/reduce_scatter | solution.py:242
  424.6 241.0 %all-reduce.37.cloned.1.call-start = ((), (), s32[]{:S(2)}) async-start(), calls=%async_computation.15 | async-start | bytes 7340032 | tf_op jit(solution)/shard_map/psum | solution.py:282
  439.1 18.0 %copy-start.73 = (f32[256]{0:T(256)S(1)}, f32[256]{0:T(256)}, u32[]{:S(2)}) copy-start(f32[256]{0:T(256)} %get-tuple-element.380) | copy-start | bytes 3076
  457.0 65.9 %copy-start.45 = (f32[512]{0:T(512)S(1)}, f32[512]{0:T(512)}, u32[]{:S(2)}) copy-start(f32[512]{0:T(512)} %copy-done.44) | copy-start | bytes 6148
  457.0 86.4 %copy-start.72 = (f32[256]{0:T(256)S(1)}, f32[256]{0:T(256)}, u32[]{:S(2)}) copy-start(f32[256]{0:T(256)} %get-tuple-element.311) | copy-start | bytes 3076
  457.0 107.7 %copy-start.30 = (f32[256,512]{1,0:T(8,128)S(1)}, f32[256,512]{1,0:T(8,128)}, u32[]{:S(2)}) copy-start(f32[256,512]{1,0:T(8,128)} %param.21) | copy-start | bytes 1572868
  457.0 107.7 %copy-start.52 = (f32[256]{0:T(256)S(1)}, f32[256]{0:T(256)}, u32[]{:S(2)}) copy-start(f32[256]{0:T(256)} %copy-done.51) | copy-start | bytes 3076
  457.6 107.0 %copy-start.14 = (f32[256,1024]{1,0:T(8,128)S(1)}, f32[256,1024]{1,0:T(8,128)}, u32[]{:S(2)}) copy-start(f32[256,1024]{1,0:T(8,128)} %copy-done.13) | copy-start | bytes 3145732
  (50 other events, 139.8 us)
Sparse Core Ops, SparseCore 0:
  11.4 19.4 all-gather.5
  33.0 16.6 all-gather.9
  52.0 77.8 reduce-scatter.4
  132.0 31.9 reduce-scatter.8
  273.5 40.0 all-reduce.30
  317.8 40.1 all-reduce.32
  360.1 21.2 all-gather.7
  382.9 33.4 all-gather.11
  418.8 36.2 all-reduce.34
  457.5 31.6 reduce-scatter.6
  491.7 31.1 reduce-scatter.10
  526.5 139.0 all-reduce.36
